TPU v7x, 32 devices: a whole 2x2x4 slice. The times are simulated.
32 devices in a mesh: clip: 2 (over y), frame: 4 (over x, core), tensor: 4 (over z).
Axes of the slice: x: 2, y: 2, z: 4, core: 2. Of those that a mesh axis runs over, the one named last changes fastest.
Arguments:
- x_in: bfloat16 [2, 16, 256, 1152], P('clip', 'frame', 'tensor'), may hold values from -6 to 6
- cond: bfloat16 [2, 1152], P('clip'), may hold values from -6 to 6
- mod_weight_one: float32 [1152, 6, 1152], P(('clip', 'frame'), None, 'tensor'), may hold values from -0.1875 to 0.1875
- qkv_weight_one: float32 [1152, 3, 1152], P(('clip', 'frame'), None, 'tensor'), may hold values from -0.1875 to 0.1875
- attn_out_one: float32 [1152, 1152], P('tensor', ('clip', 'frame')), may hold values from -0.75 to 0.75
- mlp_up_one: float32 [1152, 4608], P(('clip', 'frame'), 'tensor'), may hold values from -0.1875 to 0.1875
- mlp_down_one: float32 [4608, 1152], P('tensor', ('clip', 'frame')), may hold values from -0.09375 to 0.09375
- mod_weight_two: float32 [1152, 6, 1152], P(('clip', 'frame'), None, 'tensor'), may hold values from -0.1875 to 0.1875
- qkv_weight_two: float32 [1152, 3, 1152], P(('clip', 'frame'), None, 'tensor'), may hold values from -0.1875 to 0.1875
- attn_out_two: float32 [1152, 1152], P('tensor', ('clip', 'frame')), may hold values from -0.375 to 0.375
- mlp_up_two: float32 [1152, 4608], P(('clip', 'frame'), 'tensor'), may hold values from -0.1875 to 0.1875
- mlp_down_two: float32 [4608, 1152], P('tensor', ('clip', 'frame')), may hold values from -0.09375 to 0.09375
- out_cotangent: bfloat16 [2, 16, 256, 1152], P('clip', 'frame', 'tensor'), may hold values from -6 to 6
Outputs:
- layer_out: bfloat16 [2, 16, 256, 1152], P('clip', 'frame', 'tensor')
- input_grad: float32 [2, 16, 256, 1152], P('clip', 'frame', 'tensor')
- cond_grad: float32 [2, 1152], P('clip')
- grad_mod_one: float32 [1152, 6, 1152], P(('clip', 'frame'), None, 'tensor')
- grad_qkv_one: float32 [1152, 3, 1152], P(('clip', 'frame'), None, 'tensor')
- grad_attn_one: float32 [1152, 1152], P('tensor', ('clip', 'frame'))
- grad_up_one: float32 [1152, 4608], P(('clip', 'frame'), 'tensor')
- grad_down_one: float32 [4608, 1152], P('tensor', ('clip', 'frame'))
- grad_mod_two: float32 [1152, 6, 1152], P(('clip', 'frame'), None, 'tensor')
- grad_qkv_two: float32 [1152, 3, 1152], P(('clip', 'frame'), None, 'tensor')
- grad_attn_two: float32 [1152, 1152], P('tensor', ('clip', 'frame'))
- grad_up_two: float32 [1152, 4608], P(('clip', 'frame'), 'tensor')
- grad_down_two: float32 [4608, 1152], P('tensor', ('clip', 'frame'))
All inputs are finite; a program needn't handle non-finite values.
Results may differ from a plain program's by a relative error of at most 0.02.
Values may be sent and summed in bfloat16 or wider, within the bound.
No kernel may reach another device: no remote copies, remote signals or barrier semaphores. Data moves between devices by JAX's collectives and lax.ppermute only.
A program may use at most 192 MiB of HBM per device.

v0:
```python
import jax
import jax.numpy as jnp
from jax import lax
from jax.sharding import PartitionSpec as P

HD = 72
HIGHEST_PRECISION = lax.Precision.HIGHEST
SCORE_FORMS = {True: "cfphe,cfqhe->cfhpq", False: "cfphe,cgphe->cphfg"}
APPLY_FORMS = {True: "cfhpq,cfqhe->cfphe", False: "cphfg,cgphe->cfphe"}
BACK_FORMS = {True: "cfhpq,cfphe->cfqhe", False: "cphfg,cfphe->cgphe"}
GELU_COEFF = 0.7978845608028654
CUBIC_COEFF = 0.044715


def layer_norm(stream):
    centre = stream - jnp.mean(stream, axis=-1, keepdims=True)
    inv_scale = lax.rsqrt(jnp.mean(centre * centre, axis=-1, keepdims=True) + 1e-06)
    return (centre * inv_scale, inv_scale)


def norm_back(normed, inv_scale, upstream):
    return inv_scale * (
        upstream
        - jnp.mean(upstream, axis=-1, keepdims=True)
        - normed * jnp.mean(upstream * normed, axis=-1, keepdims=True)
    )


def gelu_tanh(inputs):
    return (
        0.5
        * inputs
        * (1.0 + jnp.tanh(GELU_COEFF * (inputs + CUBIC_COEFF * inputs * inputs * inputs)))
    )


def gelu_slope(inputs):
    tangent = jnp.tanh(GELU_COEFF * (inputs + CUBIC_COEFF * inputs * inputs * inputs))
    return 0.5 * (1.0 + tangent) + 0.5 * inputs * (1.0 - tangent * tangent) * GELU_COEFF * (
        1.0 + 3.0 * CUBIC_COEFF * inputs * inputs
    )


def choose(modulation, column):
    return modulation[:, column][:, None, None, :]


def split_heads(projected):
    leading = projected.shape[:3]
    row_width = projected.shape[-1]
    head_count = row_width // HD
    queries = projected[:, :, :, 0].reshape(leading + (head_count, HD))
    key_rows = projected[:, :, :, 1].reshape(leading + (head_count, HD))
    values = projected[:, :, :, 2].reshape(leading + (head_count, HD))
    return (queries, key_rows, values, leading, row_width)


def attend(projected, spatial):
    queries, key_rows, values, leading, row_width = split_heads(projected)
    scores = jnp.einsum(
        SCORE_FORMS[spatial], queries, key_rows, preferred_element_type=jnp.float32
    ) * HD ** (-0.5)
    highest = jnp.max(scores, axis=-1, keepdims=True)
    expo = jnp.exp(scores - highest)
    denominator = jnp.sum(expo, axis=-1, keepdims=True)
    probs = (expo / denominator).astype(jnp.bfloat16)
    log_total = highest + jnp.log(denominator)
    attended = jnp.einsum(APPLY_FORMS[spatial], probs, values, preferred_element_type=jnp.float32)
    return (attended.reshape(leading + (row_width,)).astype(jnp.bfloat16), log_total)


def attend_back(projected, log_total, d_attended, spatial):
    queries, key_rows, values, leading, row_width = split_heads(projected)
    scale_factor = HD ** (-0.5)
    scores = (
        jnp.einsum(SCORE_FORMS[spatial], queries, key_rows, preferred_element_type=jnp.float32)
        * scale_factor
    )
    probs = jnp.exp(scores - log_total)
    upstream = d_attended.reshape(leading + (row_width // HD, HD))
    d_probs = jnp.einsum(SCORE_FORMS[spatial], upstream, values, preferred_element_type=jnp.float32)
    d_values = jnp.einsum(
        BACK_FORMS[spatial],
        probs.astype(jnp.bfloat16),
        upstream,
        preferred_element_type=jnp.float32,
    )
    row_inner = jnp.sum(probs * d_probs, axis=-1, keepdims=True)
    d_scores = (probs * (d_probs - row_inner)).astype(jnp.bfloat16)
    d_queries = (
        jnp.einsum(APPLY_FORMS[spatial], d_scores, key_rows, preferred_element_type=jnp.float32)
        * scale_factor
    )
    d_keys = (
        jnp.einsum(BACK_FORMS[spatial], d_scores, queries, preferred_element_type=jnp.float32)
        * scale_factor
    )
    stacked = jnp.stack([d_queries, d_keys, d_values], axis=3)
    return stacked.reshape(leading + (3, row_width)).astype(jnp.bfloat16)


def fetch_weights(weights):
    cast = tuple((weight.astype(jnp.bfloat16) for weight in weights))
    return (
        lax.all_gather(cast[0], ("clip", "frame"), axis=0, tiled=True),
        lax.all_gather(cast[1], ("clip", "frame"), axis=0, tiled=True),
        lax.all_gather(cast[2], ("clip", "frame"), axis=1, tiled=True),
        lax.all_gather(cast[3], ("clip", "frame"), axis=0, tiled=True),
        lax.all_gather(cast[4], ("clip", "frame"), axis=1, tiled=True),
    )


def backward_weights(weights):
    cast = tuple((weight.astype(jnp.bfloat16) for weight in weights))
    return (
        lax.all_gather(cast[0], ("clip", "frame"), axis=0, tiled=True),
        lax.all_gather(cast[1], ("clip", "frame"), axis=0, tiled=True),
        lax.all_gather(cast[2], ("clip", "frame"), axis=1, tiled=True),
        lax.all_gather(cast[3], ("clip", "frame"), axis=0, tiled=True),
        lax.all_gather(cast[4], ("clip", "frame"), axis=1, tiled=True),
    )


def spread_rows(rows):
    return lax.all_gather(rows, "tensor", axis=2, tiled=True)


def collect_rows(term):
    return lax.psum_scatter(term, "tensor", scatter_dimension=2, tiled=True)


def attention_output(attended, attn_weight):
    return collect_rows(
        jnp.einsum("cfpz,zd->cfpd", attended, attn_weight, preferred_element_type=jnp.float32)
    )


def layer_forward(stream, silu_cond, gathered, spatial):
    mod_weight, qkv_weight, attn_weight, up_weight, down_weight = gathered
    partial_value = jnp.einsum(
        "cd,dkz->ckz", silu_cond, mod_weight, preferred_element_type=jnp.float32
    )
    modulation = lax.all_gather(partial_value, "tensor", axis=2, tiled=True)
    normed, inv_scale = layer_norm(stream)
    modulated = (normed * (1.0 + choose(modulation, 1)) + choose(modulation, 0)).astype(
        jnp.bfloat16
    )
    gathered_rows = spread_rows(modulated)
    projected = jnp.einsum(
        "cfpd,dkz->cfpkz", gathered_rows, qkv_weight, preferred_element_type=jnp.float32
    ).astype(jnp.bfloat16)
    if spatial:
        project_held = projected
        attended, log_total = attend(project_held, True)
    else:
        project_held = lax.all_to_all(projected, "frame", split_axis=2, concat_axis=1, tiled=True)
        placed, log_total = attend(project_held, False)
        attended = lax.all_to_all(placed, "frame", split_axis=1, concat_axis=2, tiled=True)
    branch_attn = attention_output(attended, attn_weight)
    middle = stream + choose(modulation, 2) * branch_attn
    normed_mlp, inv_mlp = layer_norm(middle)
    modulated_mlp = (normed_mlp * (1.0 + choose(modulation, 4)) + choose(modulation, 3)).astype(
        jnp.bfloat16
    )
    gathered_mlp = spread_rows(modulated_mlp)
    hidden_pre = jnp.einsum(
        "cfpd,dz->cfpz", gathered_mlp, up_weight, preferred_element_type=jnp.float32
    )
    hidden_act = gelu_tanh(hidden_pre).astype(jnp.bfloat16)
    branch_mlp = collect_rows(
        jnp.einsum("cfpz,zd->cfpd", hidden_act, down_weight, preferred_element_type=jnp.float32)
    )
    result = middle + choose(modulation, 5) * branch_mlp
    stored = (
        modulation,
        normed,
        inv_scale,
        gathered_rows,
        project_held,
        log_total,
        attended,
        branch_attn,
        normed_mlp,
        inv_mlp,
        gathered_mlp,
        hidden_pre,
        hidden_act,
        branch_mlp,
    )
    return (result, stored)


def layer_backward(upstream, silu_cond, gathered, stored, spatial):
    mod_weight, qkv_weight, attn_weight, up_weight, down_weight = gathered
    (
        modulation,
        normed,
        inv_scale,
        gathered_rows,
        project_held,
        log_total,
        attended,
        branch_attn,
        normed_mlp,
        inv_mlp,
        gathered_mlp,
        hidden_pre,
        hidden_act,
        branch_mlp,
    ) = stored
    d_branch_mlp = (upstream * choose(modulation, 5)).astype(jnp.bfloat16)
    d_gate_mlp = jnp.sum(upstream * branch_mlp, axis=(1, 2))
    d_branch_all = spread_rows(d_branch_mlp)
    grad_down = jnp.einsum(
        "cfpz,cfpd->zd", hidden_act, d_branch_all, preferred_element_type=jnp.float32
    )
    d_act = jnp.einsum(
        "cfpd,zd->cfpz", d_branch_all, down_weight, preferred_element_type=jnp.float32
    )
    d_pre = (d_act * gelu_slope(hidden_pre)).astype(jnp.bfloat16)
    grad_up = jnp.einsum("cfpd,cfpz->dz", gathered_mlp, d_pre, preferred_element_type=jnp.float32)
    d_mod_mlp = collect_rows(
        jnp.einsum("cfpz,dz->cfpd", d_pre, up_weight, preferred_element_type=jnp.float32)
    )
    d_shift_mlp = jnp.sum(d_mod_mlp, axis=(1, 2))
    d_scale_mlp = jnp.sum(d_mod_mlp * normed_mlp, axis=(1, 2))
    d_middle = upstream + norm_back(normed_mlp, inv_mlp, d_mod_mlp * (1.0 + choose(modulation, 4)))
    d_branch_attn = (d_middle * choose(modulation, 2)).astype(jnp.bfloat16)
    d_gate_attn = jnp.sum(d_middle * branch_attn, axis=(1, 2))
    d_attn_all = spread_rows(d_branch_attn)
    grad_attn = jnp.einsum(
        "cfpz,cfpd->zd", attended, d_attn_all, preferred_element_type=jnp.float32
    )
    d_attended = jnp.einsum(
        "cfpd,zd->cfpz", d_attn_all, attn_weight, preferred_element_type=jnp.float32
    ).astype(jnp.bfloat16)
    if spatial:
        d_projected = attend_back(project_held, log_total, d_attended, True)
    else:
        d_placed = lax.all_to_all(d_attended, "frame", split_axis=2, concat_axis=1, tiled=True)
        d_projected = lax.all_to_all(
            attend_back(project_held, log_total, d_placed, False),
            "frame",
            split_axis=1,
            concat_axis=2,
            tiled=True,
        )
    grad_qkv = jnp.einsum(
        "cfpd,cfpkz->dkz", gathered_rows, d_projected, preferred_element_type=jnp.float32
    )
    d_modulated = collect_rows(
        jnp.einsum("cfpkz,dkz->cfpd", d_projected, qkv_weight, preferred_element_type=jnp.float32)
    )
    d_shift_attn = jnp.sum(d_modulated, axis=(1, 2))
    d_scale_attn = jnp.sum(d_modulated * normed, axis=(1, 2))
    d_stream = d_middle + norm_back(normed, inv_scale, d_modulated * (1.0 + choose(modulation, 1)))
    d_modulation = jnp.stack(
        [d_shift_attn, d_scale_attn, d_gate_attn, d_shift_mlp, d_scale_mlp, d_gate_mlp], axis=1
    )
    d_mod_own = lax.psum_scatter(d_modulation, "tensor", scatter_dimension=2, tiled=True)
    grad_mod = jnp.einsum(
        "cd,ckz->dkz", silu_cond.astype(jnp.float32), d_mod_own, precision=HIGHEST_PRECISION
    )
    d_silu = jnp.einsum(
        "ckz,dkz->cd", d_mod_own, mod_weight.astype(jnp.float32), precision=HIGHEST_PRECISION
    )
    grads = (
        lax.psum_scatter(
            grad_mod.astype(jnp.bfloat16), ("clip", "frame"), scatter_dimension=0, tiled=True
        ).astype(jnp.float32),
        lax.psum_scatter(
            grad_qkv.astype(jnp.bfloat16), ("clip", "frame"), scatter_dimension=0, tiled=True
        ).astype(jnp.float32),
        lax.psum_scatter(
            grad_attn.astype(jnp.bfloat16), ("clip", "frame"), scatter_dimension=1, tiled=True
        ).astype(jnp.float32),
        lax.psum_scatter(
            grad_up.astype(jnp.bfloat16), ("clip", "frame"), scatter_dimension=0, tiled=True
        ).astype(jnp.float32),
        lax.psum_scatter(
            grad_down.astype(jnp.bfloat16), ("clip", "frame"), scatter_dimension=1, tiled=True
        ).astype(jnp.float32),
    )
    return (d_stream, d_silu, grads)


def local(
    x_in,
    cond,
    mod_weight_one,
    qkv_weight_one,
    attn_out_one,
    mlp_up_one,
    mlp_down_one,
    mod_weight_two,
    qkv_weight_two,
    attn_out_two,
    mlp_up_two,
    mlp_down_two,
    out_cotangent,
):
    weights_first = (mod_weight_one, qkv_weight_one, attn_out_one, mlp_up_one, mlp_down_one)
    weights_second = (mod_weight_two, qkv_weight_two, attn_out_two, mlp_up_two, mlp_down_two)
    cond_float = cond.astype(jnp.float32)
    silu_cond = jax.nn.silu(cond_float).astype(jnp.bfloat16)
    gathered_first = fetch_weights(weights_first)
    middle_stream, stored_first = layer_forward(
        x_in.astype(jnp.float32), silu_cond, gathered_first, True
    )
    gathered_second = fetch_weights(weights_second)
    result, stored_second = layer_forward(middle_stream, silu_cond, gathered_second, False)
    back_second = backward_weights(weights_second)
    d_middle_stream, d_silu_second, grads_second = layer_backward(
        out_cotangent.astype(jnp.float32), silu_cond, back_second, stored_second, False
    )
    back_first = backward_weights(weights_first)
    input_grad, d_silu_first, grads_first = layer_backward(
        d_middle_stream, silu_cond, back_first, stored_first, True
    )
    d_silu_total = lax.psum(d_silu_first + d_silu_second, ("frame", "tensor"))
    sigmoid_cond = jax.nn.sigmoid(cond_float)
    cond_grad = d_silu_total * (sigmoid_cond * (1.0 + cond_float * (1.0 - sigmoid_cond)))
    return (
        result.astype(jnp.bfloat16),
        input_grad,
        cond_grad,
        grads_first[0],
        grads_first[1],
        grads_first[2],
        grads_first[3],
        grads_first[4],
        grads_second[0],
        grads_second[1],
        grads_second[2],
        grads_second[3],
        grads_second[4],
    )


def solution(mesh):
    return jax.shard_map(
        local,
        mesh=mesh,
        in_specs=(
            P("clip", "frame", "tensor", None),
            P("clip", None),
            P(("clip", "frame"), None, "tensor"),
            P(("clip", "frame"), None, "tensor"),
            P("tensor", ("clip", "frame")),
            P(("clip", "frame"), "tensor"),
            P("tensor", ("clip", "frame")),
            P(("clip", "frame"), None, "tensor"),
            P(("clip", "frame"), None, "tensor"),
            P("tensor", ("clip", "frame")),
            P(("clip", "frame"), "tensor"),
            P("tensor", ("clip", "frame")),
            P("clip", "frame", "tensor", None),
        ),
        out_specs=(
            P("clip", "frame", "tensor", None),
            P("clip", "frame", "tensor", None),
            P("clip", None),
            P(("clip", "frame"), None, "tensor"),
            P(("clip", "frame"), None, "tensor"),
            P("tensor", ("clip", "frame")),
            P(("clip", "frame"), "tensor"),
            P("tensor", ("clip", "frame")),
            P(("clip", "frame"), None, "tensor"),
            P(("clip", "frame"), None, "tensor"),
            P("tensor", ("clip", "frame")),
            P(("clip", "frame"), "tensor"),
            P("tensor", ("clip", "frame")),
        ),
        check_vma=False,
    )
```

profile of v0, /device:TPU:0, one launch (start us, length us, event | category | flops | bytes accessed | tf_op | source)
XLA Modules:
  0.0 2178.5 jit_solution(7276182978386951180)
XLA Ops:
  11.7 43.0 %all-gather.21.cloned.1.call-done = bf16[1152,6,288]{2,0,1:T(8,128)(2,1)} async-done(((bf16[144,6,288]{2,0,1:T(8,128)(2,1)}), bf16[1152,6,288]{2,0,1:T(8,128)(2,1)}) %all-gather.21.cloned.1.call-update) | async-done | bytes 3981328 | tf_op jit(solution)/shard_map/all_gather | solution.py:105
  89.8 52.6 %all-gather.23.cloned.1.call-done = bf16[1,4,256,1152]{3,2,1,0:T(8,128)(2,1)} async-done(((bf16[1,4,64,1152]{3,2,1,0:T(8,128)(2,1)}), bf16[1,4,256,1152]{3,2,1,0:T(8,128)(2,1)}) %all-gather.23.cloned.1.call-update) | async-done | bytes 2359312 | tf_op jit(solution)/shard_map/all_gather | solution.py:125
  156.9 82.4 %reduce-scatter.25.cloned.1.call-done = f32[1,4,64,1152]{3,2,1,0:T(8,128)} async-done(((f32[1,4,256,1152]{3,2,1,0:T(8,128)}), f32[1,4,64,1152]{3,2,1,0:T(8,128)}) %reduce-scatter.25.cloned.1.call-update) | async-done | bytes 1179664 | tf_op jit(solution)/shard_map/reduce_scatter | solution.py:129
  246.0 26.4 %all-gather.29.cloned.1.call-done = bf16[1152,1152]{1,0:T(8,128)(2,1)} async-done(((bf16[144,1152]{1,0:T(8,128)(2,1)}), bf16[1152,1152]{1,0:T(8,128)(2,1)}) %all-gather.29.cloned.1.call-update) | async-done | bytes 2654224 | tf_op jit(solution)/shard_map/all_gather | solution.py:108
  272.4 52.5 %all-gather.27.cloned.1.call-done = bf16[1,4,256,1152]{3,2,1,0:T(8,128)(2,1)} async-done(((bf16[1,4,64,1152]{3,2,1,0:T(8,128)(2,1)}), bf16[1,4,256,1152]{3,2,1,0:T(8,128)(2,1)}) %all-gather.27.cloned.1.call-update) | async-done | bytes 2359312 | tf_op jit(solution)/shard_map/all_gather | solution.py:125
  368.0 32.4 %all-gather.33.cloned.1.call-done = bf16[1152,6,288]{2,0,1:T(8,128)(2,1)} async-done(((bf16[144,6,288]{2,0,1:T(8,128)(2,1)}), bf16[1152,6,288]{2,0,1:T(8,128)(2,1)}) %all-gather.33.cloned.1.call-update) | async-done | bytes 3981328 | tf_op jit(solution)/shard_map/all_gather | solution.py:105
  418.2 70.3 %reduce-scatter.27.cloned.1.call-done = f32[1,4,64,1152]{3,2,1,0:T(8,128)} async-done(((f32[1,4,256,1152]{3,2,1,0:T(8,128)}), f32[1,4,64,1152]{3,2,1,0:T(8,128)}) %reduce-scatter.27.cloned.1.call-update) | async-done | bytes 1179664 | tf_op jit(solution)/shard_map/reduce_scatter | solution.py:129
  491.4 30.1 %all-gather.37.cloned.1.call-done = bf16[1152,3,288]{2,0,1:T(8,128)(2,1)} async-done(((bf16[144,3,288]{2,0,1:T(8,128)(2,1)}), bf16[1152,3,288]{2,0,1:T(8,128)(2,1)}) %all-gather.37.cloned.1.call-update) | async-done | bytes 1990672 | tf_op jit(solution)/shard_map/all_gather | solution.py:106
  521.5 52.6 %all-gather.35.cloned.1.call-done = bf16[1,4,256,1152]{3,2,1,0:T(8,128)(2,1)} async-done(((bf16[1,4,64,1152]{3,2,1,0:T(8,128)(2,1)}), bf16[1,4,256,1152]{3,2,1,0:T(8,128)(2,1)}) %all-gather.35.cloned.1.call-update) | async-done | bytes 2359312 | tf_op jit(solution)/shard_map/all_gather | solution.py:125
  584.2 31.2 %all_to_all.63 = bf16[1,4,256,3,288]{4,1,3,0,2:T(4,128)(2,1)S(1)} all-to-all(bf16[1,4,256,3,288]{4,1,3,0,2:T(4,128)(2,1)S(1)} %copy.135), channel_id=1, replica_groups=mesh['clip'=2,'frame'=4,'tensor'=4] {'frame'}, dimensions={2} | all-to-all | bytes 3538944 | tf_op jit(solution)/shard_map/all_to_all | solution.py:156
  662.3 81.6 %reduce-scatter.29.cloned.1.call-done = f32[1,4,64,1152]{3,2,1,0:T(8,128)} async-done(((f32[1,4,256,1152]{3,2,1,0:T(8,128)}), f32[1,4,64,1152]{3,2,1,0:T(8,128)}) %reduce-scatter.29.cloned.1.call-update) | async-done | bytes 1179664 | tf_op jit(solution)/shard_map/reduce_scatter | solution.py:129
  776.6 52.5 %all-gather.39.cloned.1.call-done = bf16[1,4,256,1152]{3,2,1,0:T(8,128)(2,1)} async-done(((bf16[1,4,64,1152]{3,2,1,0:T(8,128)(2,1)}), bf16[1,4,256,1152]{3,2,1,0:T(8,128)(2,1)}) %all-gather.39.cloned.1.call-update) | async-done | bytes 2359312 | tf_op jit(solution)/shard_map/all_gather | solution.py:125
  860.5 52.5 %all-gather.45.cloned.1.call-done = bf16[1,4,256,1152]{3,2,1,0:T(8,128)(2,1)} async-done(((bf16[1,4,64,1152]{3,2,1,0:T(8,128)(2,1)}), bf16[1,4,256,1152]{3,2,1,0:T(8,128)(2,1)}) %all-gather.45.cloned.1.call-update) | async-done | bytes 2359312 | tf_op jit(solution)/shard_map/all_gather | solution.py:125
  936.8 74.7 %reduce-scatter.33.cloned.1.call-done = f32[1,4,64,1152]{3,2,1,0:T(8,128)} async-done(((f32[1,4,256,1152]{3,2,1,0:T(8,128)}), f32[1,4,64,1152]{3,2,1,0:T(8,128)}) %reduce-scatter.33.cloned.1.call-update) | async-done | bytes 1179664 | tf_op jit(solution)/shard_map/reduce_scatter | solution.py:129
  1014.2 85.2 %reduce-scatter.31.cloned.1.call-done = f32[1,4,64,1152]{3,2,1,0:T(8,128)} async-done(((f32[1,4,256,1152]{3,2,1,0:T(8,128)}), f32[1,4,64,1152]{3,2,1,0:T(8,128)}) %reduce-scatter.31.cloned.1.call-update) | async-done | bytes 1179664 | tf_op jit(solution)/shard_map/reduce_scatter | solution.py:129
  1106.1 51.1 %all-gather.47.cloned.1.call-done = bf16[1,4,256,1152]{3,2,1,0:T(8,128)(2,1)} async-done(((bf16[1,4,64,1152]{3,2,1,0:T(8,128)(2,1)}), bf16[1,4,256,1152]{3,2,1,0:T(8,128)(2,1)}) %all-gather.47.cloned.1.call-update) | async-done | bytes 2359312 | tf_op jit(solution)/shard_map/all_gather | solution.py:125
  1204.7 31.1 %all_to_all.64 = bf16[1,16,64,3,288]{4,2,3,0,1:T(8,128)(2,1)S(1)} all-to-all(bf16[1,16,64,3,288]{4,2,3,0,1:T(8,128)(2,1)S(1)} %copy.158), channel_id=1, replica_groups=mesh['clip'=2,'frame'=4,'tensor'=4] {'frame'}, dimensions={1} | all-to-all | bytes 3538944 | tf_op jit(solution)/shard_map/all_to_all | solution.py:241
  1243.8 83.3 %reduce-scatter.35.cloned.1.call-done = f32[1,4,64,1152]{3,2,1,0:T(8,128)} async-done(((f32[1,4,256,1152]{3,2,1,0:T(8,128)}), f32[1,4,64,1152]{3,2,1,0:T(8,128)}) %reduce-scatter.35.cloned.1.call-update) | async-done | bytes 1179664 | tf_op jit(solution)/shard_map/reduce_scatter | solution.py:129
  1333.0 51.1 %all-gather.49.cloned.1.call-done = bf16[1,4,256,1152]{3,2,1,0:T(8,128)(2,1)} async-done(((bf16[1,4,64,1152]{3,2,1,0:T(8,128)(2,1)}), bf16[1,4,256,1152]{3,2,1,0:T(8,128)(2,1)}) %all-gather.49.cloned.1.call-update) | async-done | bytes 2359312 | tf_op jit(solution)/shard_map/all_gather | solution.py:125
  1398.4 84.2 %reduce-scatter.37.cloned.1.call-done = f32[1,4,64,1152]{3,2,1,0:T(8,128)} async-done(((f32[1,4,256,1152]{3,2,1,0:T(8,128)}), f32[1,4,64,1152]{3,2,1,0:T(8,128)}) %reduce-scatter.37.cloned.1.call-update) | async-done | bytes 1179664 | tf_op jit(solution)/shard_map/reduce_scatter | solution.py:129
  1488.7 50.8 %all-gather.51.cloned.1.call-done = bf16[1,4,256,1152]{3,2,1,0:T(8,128)(2,1)} async-done(((bf16[1,4,64,1152]{3,2,1,0:T(8,128)(2,1)}), bf16[1,4,256,1152]{3,2,1,0:T(8,128)(2,1)}) %all-gather.51.cloned.1.call-update) | async-done | bytes 2359312 | tf_op jit(solution)/shard_map/all_gather | solution.py:125
  1556.4 82.2 %reduce-scatter.39.cloned.1.call-done = f32[1,4,64,1152]{3,2,1,0:T(8,128)} async-done(((f32[1,4,256,1152]{3,2,1,0:T(8,128)}), f32[1,4,64,1152]{3,2,1,0:T(8,128)}) %reduce-scatter.39.cloned.1.call-update) | async-done | bytes 1179664 | tf_op jit(solution)/shard_map/reduce_scatter | solution.py:129
  1707.4 25.1 %reduce-scatter.57.cloned.1.call-done = bf16[144,1152]{1,0:T(8,128)(2,1)} async-done(((bf16[1152,1152]{1,0:T(8,128)(2,1)}), bf16[144,1152]{1,0:T(8,128)(2,1)}) %reduce-scatter.57.cloned.1.call-update) | async-done | bytes 331792 | tf_op jit(solution)/shard_map/reduce_scatter | solution.py:277
  1734.3 45.8 %reduce-scatter.59.cloned.1.call-done = bf16[1152,144]{0,1:T(8,128)(2,1)} async-done(((bf16[1152,1152]{0,1:T(8,128)(2,1)}), bf16[1152,144]{0,1:T(8,128)(2,1)}) %reduce-scatter.59.cloned.1.call-update) | async-done | bytes 331792 | tf_op jit(solution)/shard_map/reduce_scatter | solution.py:280
  1782.0 37.1 %reduce-scatter.55.cloned.1.call-done = bf16[288,144]{0,1:T(8,128)(2,1)} async-done(((bf16[288,1152]{0,1:T(8,128)(2,1)}), bf16[288,144]{0,1:T(8,128)(2,1)}) %reduce-scatter.55.cloned.1.call-update) | async-done | bytes 82960 | tf_op jit(solution)/shard_map/reduce_scatter | solution.py:274
  1820.7 45.9 %reduce-scatter.53.cloned.1.call-done = bf16[144,3,288]{2,0,1:T(8,128)(2,1)} async-done(((bf16[1152,3,288]{2,0,1:T(8,128)(2,1)}), bf16[144,3,288]{2,0,1:T(8,128)(2,1)}) %reduce-scatter.53.cloned.1.call-update) | async-done | bytes 248848 | tf_op jit(solution)/shard_map/reduce_scatter | solution.py:271
  1875.2 38.7 %reduce-scatter.47.cloned.1.call-done = bf16[144,1152]{1,0:T(8,128)(2,1)} async-done(((bf16[1152,1152]{1,0:T(8,128)(2,1)}), bf16[144,1152]{1,0:T(8,128)(2,1)}) %reduce-scatter.47.cloned.1.call-update) | async-done | bytes 331792 | tf_op jit(solution)/shard_map/reduce_scatter | solution.py:277
  1915.8 45.8 %reduce-scatter.49.cloned.1.call-done = bf16[1152,144]{0,1:T(8,128)(2,1)} async-done(((bf16[1152,1152]{0,1:T(8,128)(2,1)}), bf16[1152,144]{0,1:T(8,128)(2,1)}) %reduce-scatter.49.cloned.1.call-update) | async-done | bytes 331792 | tf_op jit(solution)/shard_map/reduce_scatter | solution.py:280
  1963.4 36.9 %reduce-scatter.45.cloned.1.call-done = bf16[288,144]{0,1:T(8,128)(2,1)} async-done(((bf16[288,1152]{0,1:T(8,128)(2,1)}), bf16[288,144]{0,1:T(8,128)(2,1)}) %reduce-scatter.45.cloned.1.call-update) | async-done | bytes 82960 | tf_op jit(solution)/shard_map/reduce_scatter | solution.py:274
  2001.9 46.1 %reduce-scatter.43.cloned.1.call-done = bf16[144,3,288]{2,0,1:T(8,128)(2,1)} async-done(((bf16[1152,3,288]{2,0,1:T(8,128)(2,1)}), bf16[144,3,288]{2,0,1:T(8,128)(2,1)}) %reduce-scatter.43.cloned.1.call-update) | async-done | bytes 248848 | tf_op jit(solution)/shard_map/reduce_scatter | solution.py:271
  2058.1 34.4 %psum.7 = f32[1,1152]{1,0:T(1,128)S(1)} all-reduce(f32[1,1152]{1,0:T(1,128)S(1)} %add.296), channel_id=1, replica_groups=mesh['clip'=2,'frame'=4,'tensor'=4] {'frame','tensor'}, use_global_device_ids=true, to_apply=%region_44.45 | all-reduce | flops 1152 | bytes 9216 | tf_op jit(solution)/shard_map/psum | solution.py:320
  2111.1 58.4 %reduce-scatter.51.cloned.1.call-done = bf16[144,6,288]{2,0,1:T(8,128)(2,1)} async-done(((bf16[1152,6,288]{2,0,1:T(8,128)(2,1)}), bf16[144,6,288]{2,0,1:T(8,128)(2,1)}) %reduce-scatter.51.cloned.1.call-update) | async-done | bytes 497680 | tf_op jit(solution)/shard_map/reduce_scatter | solution.py:268
  (424 shorter events, 495.0 us)
Async XLA Ops:
  10.5 132.0 %all-gather.23.cloned.1.call-start = ((), (), s32[]{:S(2)}) async-start(), calls=%async_computation.25 | async-start | bytes 2949120 | tf_op jit(solution)/shard_map/all_gather | solution.py:125
  73.1 166.2 %reduce-scatter.25.cloned.1.call-start = ((), (), s32[]{:S(2)}) async-start(), calls=%async_computation.27 | async-start | bytes 5898240 | tf_op jit(solution)/shard_map/reduce_scatter | solution.py:129
  155.0 117.4 %all-gather.29.cloned.1.call-start = ((), (), s32[]{:S(2)}) async-start(), calls=%async_computation.29 | async-start | bytes 2985984 | tf_op jit(solution)/shard_map/all_gather | solution.py:108
  156.9 168.0 %all-gather.27.cloned.1.call-start = ((), (), s32[]{:S(2)}) async-start(), calls=%async_computation.28 | async-start | bytes 2949120 | tf_op jit(solution)/shard_map/all_gather | solution.py:125
  242.2 114.2 %all-gather.31.cloned.1.call-start = ((), (), s32[]{:S(2)}) async-start(), calls=%async_computation.30 | async-start | bytes 2985984 | tf_op jit(solution)/shard_map/all_gather | solution.py:109
  243.2 157.2 %all-gather.33.cloned.1.call-start = ((), (), s32[]{:S(2)}) async-start(), calls=%async_computation.32 | async-start | bytes 5971968 | tf_op jit(solution)/shard_map/all_gather | solution.py:105
  245.5 243.0 %reduce-scatter.27.cloned.1.call-start = ((), (), s32[]{:S(2)}) async-start(), calls=%async_computation.31 | async-start | bytes 5898240 | tf_op jit(solution)/shard_map/reduce_scatter | solution.py:129
  366.0 155.5 %all-gather.37.cloned.1.call-start = ((), (), s32[]{:S(2)}) async-start(), calls=%async_computation.34 | async-start | bytes 2985984 | tf_op jit(solution)/shard_map/all_gather | solution.py:106
  367.9 206.2 %all-gather.35.cloned.1.call-start = ((), (), s32[]{:S(2)}) async-start(), calls=%async_computation.33 | async-start | bytes 2949120 | tf_op jit(solution)/shard_map/all_gather | solution.py:125
  660.4 116.2 %all-gather.41.cloned.1.call-start = ((), (), s32[]{:S(2)}) async-start(), calls=%async_computation.37 | async-start | bytes 2985984 | tf_op jit(solution)/shard_map/all_gather | solution.py:108
  662.3 166.8 %all-gather.39.cloned.1.call-start = ((), (), s32[]{:S(2)}) async-start(), calls=%async_computation.36 | async-start | bytes 2949120 | tf_op jit(solution)/shard_map/all_gather | solution.py:125
  747.5 112.9 %all-gather.43.cloned.1.call-start = ((), (), s32[]{:S(2)}) async-start(), calls=%async_computation.38 | async-start | bytes 2985984 | tf_op jit(solution)/shard_map/all_gather | solution.py:109
  749.5 163.5 %all-gather.45.cloned.1.call-start = ((), (), s32[]{:S(2)}) async-start(), calls=%async_computation.40 | async-start | bytes 2949120 | tf_op jit(solution)/shard_map/all_gather | solution.py:125
  751.5 260.0 %reduce-scatter.33.cloned.1.call-start = ((), (), s32[]{:S(2)}) async-start(), calls=%async_computation.41 | async-start | bytes 5898240 | tf_op jit(solution)/shard_map/reduce_scatter | solution.py:129
  927.3 172.2 %reduce-scatter.31.cloned.1.call-start = ((), (), s32[]{:S(2)}) async-start(), calls=%async_computation.39 | async-start | bytes 5898240 | tf_op jit(solution)/shard_map/reduce_scatter | solution.py:129
  936.8 220.4 %all-gather.47.cloned.1.call-start = ((), (), s32[]{:S(2)}) async-start(), calls=%async_computation.42 | async-start | bytes 2949120 | tf_op jit(solution)/shard_map/all_gather | solution.py:125
  1167.2 159.9 %reduce-scatter.35.cloned.1.call-start = ((), (), s32[]{:S(2)}) async-start(), calls=%async_computation.43 | async-start | bytes 5898240 | tf_op jit(solution)/shard_map/reduce_scatter | solution.py:129
  1243.8 140.3 %all-gather.49.cloned.1.call-start = ((), (), s32[]{:S(2)}) async-start(), calls=%async_computation.44 | async-start | bytes 2949120 | tf_op jit(solution)/shard_map/all_gather | solution.py:125
  1332.9 149.7 %reduce-scatter.37.cloned.1.call-start = ((), (), s32[]{:S(2)}) async-start(), calls=%async_computation.45 | async-start | bytes 5898240 | tf_op jit(solution)/shard_map/reduce_scatter | solution.py:129
  1398.3 141.2 %all-gather.51.cloned.1.call-start = ((), (), s32[]{:S(2)}) async-start(), calls=%async_computation.46 | async-start | bytes 2949120 | tf_op jit(solution)/shard_map/all_gather | solution.py:125
  1488.4 150.2 %reduce-scatter.39.cloned.1.call-start = ((), (), s32[]{:S(2)}) async-start(), calls=%async_computation.47 | async-start | bytes 5898240 | tf_op jit(solution)/shard_map/reduce_scatter | solution.py:129
  1554.3 143.7 %reduce-scatter.63.cloned.1.call-start = ((), (), s32[]{:S(2)}) async-start(), calls=%async_computation.59 | async-start | bytes 737280
  1556.2 142.8 %reduce-scatter.61.cloned.1.call-start = ((), (), s32[]{:S(2)}) async-start(), calls=%async_computation.58 | async-start | bytes 737280
  1648.9 131.2 %reduce-scatter.59.cloned.1.call-start = ((), (), s32[]{:S(2)}) async-start(), calls=%async_computation.57 | async-start | bytes 2985984 | tf_op jit(solution)/shard_map/reduce_scatter | solution.py:280
  1657.5 161.6 %reduce-scatter.55.cloned.1.call-start = ((), (), s32[]{:S(2)}) async-start(), calls=%async_computation.55 | async-start | bytes 995328 | tf_op jit(solution)/shard_map/reduce_scatter | solution.py:274
  1662.6 204.0 %reduce-scatter.53.cloned.1.call-start = ((), (), s32[]{:S(2)}) async-start(), calls=%async_computation.54 | async-start | bytes 2985984 | tf_op jit(solution)/shard_map/reduce_scatter | solution.py:271
  1669.8 244.1 %reduce-scatter.47.cloned.1.call-start = ((), (), s32[]{:S(2)}) async-start(), calls=%async_computation.51 | async-start | bytes 2985984 | tf_op jit(solution)/shard_map/reduce_scatter | solution.py:277
  1677.2 284.4 %reduce-scatter.49.cloned.1.call-start = ((), (), s32[]{:S(2)}) async-start(), calls=%async_computation.52 | async-start | bytes 2985984 | tf_op jit(solution)/shard_map/reduce_scatter | solution.py:280
  1685.4 314.9 %reduce-scatter.45.cloned.1.call-start = ((), (), s32[]{:S(2)}) async-start(), calls=%async_computation.50 | async-start | bytes 995328 | tf_op jit(solution)/shard_map/reduce_scatter | solution.py:274
  1690.5 357.5 %reduce-scatter.43.cloned.1.call-start = ((), (), s32[]{:S(2)}) async-start(), calls=%async_computation.49 | async-start | bytes 2985984 | tf_op jit(solution)/shard_map/reduce_scatter | solution.py:271
  1697.3 411.6 %reduce-scatter.41.cloned.1.call-start = ((), (), s32[]{:S(2)}) async-start(), calls=%async_computation.48 | async-start | bytes 5971968 | tf_op jit(solution)/shard_map/reduce_scatter | solution.py:268
  1706.8 462.7 %reduce-scatter.51.cloned.1.call-start = ((), (), s32[]{:S(2)}) async-start(), calls=%async_computation.53 | async-start | bytes 5971968 | tf_op jit(solution)/shard_map/reduce_scatter | solution.py:268
  (94 other events, 3726.8 us)
Sparse Core Ops, SparseCore 0:
  10.5 44.0 all-gather.20
  57.1 32.6 all-gather.24
  91.9 50.4 all-gather.22
  155.2 84.0 reduce-scatter.24
  241.6 30.7 all-gather.28
  274.4 50.4 all-gather.26
  359.0 41.3 all-gather.32
  402.7 85.7 reduce-scatter.26
  490.8 30.5 all-gather.36
  523.6 50.4 all-gather.34
  660.5 83.3 reduce-scatter.28
  745.8 30.7 all-gather.40
  778.6 50.4 all-gather.38
  862.5 50.4 all-gather.44
  927.4 84.0 reduce-scatter.32
  1013.7 85.7 reduce-scatter.30
  1106.2 50.9 all-gather.46
  1243.9 83.1 reduce-scatter.34
  1333.1 50.9 all-gather.48
  1398.5 84.0 reduce-scatter.36
  1488.5 50.9 all-gather.50
  1554.4 84.0 reduce-scatter.38
  1690.4 42.0 reduce-scatter.56
  1736.3 43.7 reduce-scatter.58
  1783.9 35.0 reduce-scatter.54
  1822.8 43.7 reduce-scatter.52
  1870.1 43.7 reduce-scatter.46
  1917.8 43.7 reduce-scatter.48
  1965.2 35.0 reduce-scatter.44
  2004.2 43.7 reduce-scatter.42
  2051.5 57.3 reduce-scatter.40
  2112.3 57.2 reduce-scatter.50
  (4 shorter events, 100.8 us)
where the time goes:
time: 2190 us; the launch traced here: 2180 us
  waiting for transfers between devices  1670 us (76%)
  matrix products  185 us (8%)
  blocking collectives  155 us (7%)
  other arithmetic  81.1 us (4%)
  local copies, waits for them, and re-layouts  56.7 us (3%)
    reduce_scatter x8, waiting for transfers between devices, collect_rows(): return lax.psum_scatter(term, 'tensor', scatter_dimension=2, tiled=True)  644 us
    all_gather x8, waiting for transfers between devices, spread_rows(): return lax.all_gather(rows, 'tensor', axis=2, tiled=True)  416 us
    reduce_scatter x2, waiting for transfers between devices, layer_backward(): lax.psum_scatter(grad_qkv.astype(jnp.bfloat16), ('clip', 'frame'), scatte...  92 us
    reduce_scatter x2, waiting for transfers between devices, layer_backward(): lax.psum_scatter(grad_down.astype(jnp.bfloat16), ('clip', 'frame'), scatt...  91.6 us
    all_gather x2, waiting for transfers between devices, fetch_weights(): lax.all_gather(cast[0], ('clip', 'frame'), axis=0, tiled=True)  75.4 us
    reduce_scatter x2, waiting for transfers between devices, layer_backward(): lax.psum_scatter(grad_mod.astype(jnp.bfloat16), ('clip', 'frame'), scatte...  74.1 us
    reduce_scatter x2, waiting for transfers between devices, layer_backward(): lax.psum_scatter(grad_attn.astype(jnp.bfloat16), ('clip', 'frame'), scatt...  74 us
    reduce_scatter x2, waiting for transfers between devices, layer_backward(): lax.psum_scatter(grad_up.astype(jnp.bfloat16), ('clip', 'frame'), scatter...  63.8 us
  transfers between devices with their start and end apart: 38, of which 35 were waited for; matrix products, arithmetic and copies ran while one was open for 8% of the time, Pallas kernels for 0%

commit v1 on v0

--- a/solution.py
+++ b/solution.py
@@ -10,6 +10,27 @@
 BACK_FORMS = {True: "cfhpq,cfphe->cfqhe", False: "cphfg,cfphe->cgphe"}
 GELU_COEFF = 0.7978845608028654
 CUBIC_COEFF = 0.044715
+
+
+def joined_along(blocks, dim):
+    blocks = jnp.moveaxis(blocks, 0, dim)
+    lengths = blocks.shape
+    return blocks.reshape(*lengths[:dim], lengths[dim] * lengths[dim + 1], *lengths[dim + 2 :])
+
+
+def doubled(value, axis):
+    size, mine = (lax.axis_size(axis), lax.axis_index(axis))
+    blocks, apart = (value[None], 1)
+    while apart < size:
+        other = lax.ppermute(blocks, axis, [(i, i ^ apart) for i in range(size)])
+        low = mine & apart == 0
+        blocks = jnp.concatenate([jnp.where(low, blocks, other), jnp.where(low, other, blocks)])
+        apart *= 2
+    return blocks
+
+
+def doubled_up(shard, axis, dim):
+    return joined_along(doubled(shard, axis), dim)
 
 
 def layer_norm(stream):
@@ -102,7 +123,7 @@
 def fetch_weights(weights):
     cast = tuple((weight.astype(jnp.bfloat16) for weight in weights))
     return (
-        lax.all_gather(cast[0], ("clip", "frame"), axis=0, tiled=True),
+        doubled_up(cast[0], ("clip", "frame"), 0),
         lax.all_gather(cast[1], ("clip", "frame"), axis=0, tiled=True),
         lax.all_gather(cast[2], ("clip", "frame"), axis=1, tiled=True),
         lax.all_gather(cast[3], ("clip", "frame"), axis=0, tiled=True),

time: 2190 us -> 2320 us (1.059)
  waiting for transfers between devices: 1670 us -> 1780 us
    ppermute x0 -> x6, waiting for transfers between devices: none -> 181 us  [doubled(): other = lax.ppermute(blocks, axis, [(i, i ^ apart) for i in range(size)])]
    reduce_scatter x8, waiting for transfers between devices: 644 us -> 574 us  [collect_rows(): return lax.psum_scatter(term, 'tensor', scatter_dimension=2, tiled=True)]
  transfers between devices with their start and end apart: 38 -> 44, of which waited for: 35 -> 39; matrix products, arithmetic and copies ran while one was open for 8% -> 7% of each run, Pallas kernels for 0% -> 0%
where the time goes in v1:
time: 2320 us; the launch traced here: 2310 us
  waiting for transfers between devices  1780 us (77%)
  matrix products  183 us (8%)
  blocking collectives  155 us (7%)
  other arithmetic  102 us (4%)
  local copies, waits for them, and re-layouts  56.5 us (2%)
    reduce_scatter x8, waiting for transfers between devices, collect_rows(): return lax.psum_scatter(term, 'tensor', scatter_dimension=2, tiled=True)  574 us
    all_gather x8, waiting for transfers between devices, spread_rows(): return lax.all_gather(rows, 'tensor', axis=2, tiled=True)  403 us
    ppermute x6, waiting for transfers between devices, doubled(): other = lax.ppermute(blocks, axis, [(i, i ^ apart) for i in range(size)])  181 us
    reduce_scatter x2, waiting for transfers between devices, layer_backward(): lax.psum_scatter(grad_qkv.astype(jnp.bfloat16), ('clip', 'frame'), scatte...  92 us
    reduce_scatter x2, waiting for transfers between devices, layer_backward(): lax.psum_scatter(grad_down.astype(jnp.bfloat16), ('clip', 'frame'), scatt...  86 us
    all_gather x2, waiting for transfers between devices, backward_weights(): lax.all_gather(cast[0], ('clip', 'frame'), axis=0, tiled=True)  82.6 us
    reduce_scatter x2, waiting for transfers between devices, layer_backward(): lax.psum_scatter(grad_mod.astype(jnp.bfloat16), ('clip', 'frame'), scatte...  76.9 us
    reduce_scatter x2, waiting for transfers between devices, layer_backward(): lax.psum_scatter(grad_attn.astype(jnp.bfloat16), ('clip', 'frame'), scatt...  74.1 us
  transfers between devices with their start and end apart: 44, of which 39 were waited for; matrix products, arithmetic and copies ran while one was open for 7% of the time, Pallas kernels for 0%

profile of v1, /device:TPU:0, one launch (start us, length us, event | category | flops | bytes accessed | tf_op | source)
XLA Modules:
  0.0 2310.1 jit_solution(11917361715559464967)
XLA Ops:
  85.1 66.3 %collective-permute-done.2 = bf16[4,144,6,288]{3,1,2,0:T(8,128)(2,1)} collective-permute-done((bf16[4,144,6,288]{3,1,2,0:T(8,128)(2,1)}, bf16[4,144,6,288]{3,1,2,0:T(8,128)(2,1)}, u32[]{:S(2)}, u32[]{:S(2)}) %collective-permute-start.2) | collective-permute-done | bytes 1990688 | tf_op jit(solution)/shard_map/ppermute | solution.py:25
  182.2 40.6 %all-gather.21.cloned.1.call-done = bf16[1,4,256,1152]{3,2,1,0:T(8,128)(2,1)} async-done(((bf16[1,4,64,1152]{3,2,1,0:T(8,128)(2,1)}), bf16[1,4,256,1152]{3,2,1,0:T(8,128)(2,1)}) %all-gather.21.cloned.1.call-update) | async-done | bytes 2359312 | tf_op jit(solution)/shard_map/all_gather | solution.py:146
  237.2 82.4 %reduce-scatter.25.cloned.1.call-done = f32[1,4,64,1152]{3,2,1,0:T(8,128)} async-done(((f32[1,4,256,1152]{3,2,1,0:T(8,128)}), f32[1,4,64,1152]{3,2,1,0:T(8,128)}) %reduce-scatter.25.cloned.1.call-update) | async-done | bytes 1179664 | tf_op jit(solution)/shard_map/reduce_scatter | solution.py:150
  324.0 28.7 %all-gather.27.cloned.1.call-done = bf16[1152,1152]{1,0:T(8,128)(2,1)} async-done(((bf16[144,1152]{1,0:T(8,128)(2,1)}), bf16[1152,1152]{1,0:T(8,128)(2,1)}) %all-gather.27.cloned.1.call-update) | async-done | bytes 2654224 | tf_op jit(solution)/shard_map/all_gather | solution.py:129
  352.7 52.5 %all-gather.25.cloned.1.call-done = bf16[1,4,256,1152]{3,2,1,0:T(8,128)(2,1)} async-done(((bf16[1,4,64,1152]{3,2,1,0:T(8,128)(2,1)}), bf16[1,4,256,1152]{3,2,1,0:T(8,128)(2,1)}) %all-gather.25.cloned.1.call-update) | async-done | bytes 2359312 | tf_op jit(solution)/shard_map/all_gather | solution.py:146
  452.2 57.8 %collective-permute-done.5 = bf16[4,144,6,288]{3,1,2,0:T(8,128)(2,1)} collective-permute-done((bf16[4,144,6,288]{3,1,2,0:T(8,128)(2,1)}, bf16[4,144,6,288]{3,1,2,0:T(8,128)(2,1)}, u32[]{:S(2)}, u32[]{:S(2)}) %collective-permute-start.5) | collective-permute-done | bytes 1990688 | tf_op jit(solution)/shard_map/ppermute | solution.py:25
  535.2 30.4 %all-gather.33.cloned.1.call-done = bf16[1152,3,288]{2,0,1:T(8,128)(2,1)} async-done(((bf16[144,3,288]{2,0,1:T(8,128)(2,1)}), bf16[1152,3,288]{2,0,1:T(8,128)(2,1)}) %all-gather.33.cloned.1.call-update) | async-done | bytes 1990672 | tf_op jit(solution)/shard_map/all_gather | solution.py:127
  565.6 52.6 %all-gather.31.cloned.1.call-done = bf16[1,4,256,1152]{3,2,1,0:T(8,128)(2,1)} async-done(((bf16[1,4,64,1152]{3,2,1,0:T(8,128)(2,1)}), bf16[1,4,256,1152]{3,2,1,0:T(8,128)(2,1)}) %all-gather.31.cloned.1.call-update) | async-done | bytes 2359312 | tf_op jit(solution)/shard_map/all_gather | solution.py:146
  628.4 31.1 %all_to_all.63 = bf16[1,4,256,3,288]{4,1,3,0,2:T(4,128)(2,1)S(1)} all-to-all(bf16[1,4,256,3,288]{4,1,3,0,2:T(4,128)(2,1)S(1)} %copy.141), channel_id=1, replica_groups=mesh['clip'=2,'frame'=4,'tensor'=4] {'frame'}, dimensions={2} | all-to-all | bytes 3538944 | tf_op jit(solution)/shard_map/all_to_all | solution.py:177
  706.4 81.5 %reduce-scatter.29.cloned.1.call-done = f32[1,4,64,1152]{3,2,1,0:T(8,128)} async-done(((f32[1,4,256,1152]{3,2,1,0:T(8,128)}), f32[1,4,64,1152]{3,2,1,0:T(8,128)}) %reduce-scatter.29.cloned.1.call-update) | async-done | bytes 1179664 | tf_op jit(solution)/shard_map/reduce_scatter | solution.py:150
  821.2 52.5 %all-gather.35.cloned.1.call-done = bf16[1,4,256,1152]{3,2,1,0:T(8,128)(2,1)} async-done(((bf16[1,4,64,1152]{3,2,1,0:T(8,128)(2,1)}), bf16[1,4,256,1152]{3,2,1,0:T(8,128)(2,1)}) %all-gather.35.cloned.1.call-update) | async-done | bytes 2359312 | tf_op jit(solution)/shard_map/all_gather | solution.py:146
  905.3 52.5 %all-gather.41.cloned.1.call-done = bf16[1,4,256,1152]{3,2,1,0:T(8,128)(2,1)} async-done(((bf16[1,4,64,1152]{3,2,1,0:T(8,128)(2,1)}), bf16[1,4,256,1152]{3,2,1,0:T(8,128)(2,1)}) %all-gather.41.cloned.1.call-update) | async-done | bytes 2359312 | tf_op jit(solution)/shard_map/all_gather | solution.py:146
  981.8 74.5 %reduce-scatter.33.cloned.1.call-done = f32[1,4,64,1152]{3,2,1,0:T(8,128)} async-done(((f32[1,4,256,1152]{3,2,1,0:T(8,128)}), f32[1,4,64,1152]{3,2,1,0:T(8,128)}) %reduce-scatter.33.cloned.1.call-update) | async-done | bytes 1179664 | tf_op jit(solution)/shard_map/reduce_scatter | solution.py:150
  1059.0 85.2 %reduce-scatter.31.cloned.1.call-done = f32[1,4,64,1152]{3,2,1,0:T(8,128)} async-done(((f32[1,4,256,1152]{3,2,1,0:T(8,128)}), f32[1,4,64,1152]{3,2,1,0:T(8,128)}) %reduce-scatter.31.cloned.1.call-update) | async-done | bytes 1179664 | tf_op jit(solution)/shard_map/reduce_scatter | solution.py:150
  1150.8 51.1 %all-gather.43.cloned.1.call-done = bf16[1,4,256,1152]{3,2,1,0:T(8,128)(2,1)} async-done(((bf16[1,4,64,1152]{3,2,1,0:T(8,128)(2,1)}), bf16[1,4,256,1152]{3,2,1,0:T(8,128)(2,1)}) %all-gather.43.cloned.1.call-update) | async-done | bytes 2359312 | tf_op jit(solution)/shard_map/all_gather | solution.py:146
  1248.6 31.2 %all_to_all.64 = bf16[1,16,64,3,288]{4,2,3,0,1:T(8,128)(2,1)S(1)} all-to-all(bf16[1,16,64,3,288]{4,2,3,0,1:T(8,128)(2,1)S(1)} %copy.164), channel_id=1, replica_groups=mesh['clip'=2,'frame'=4,'tensor'=4] {'frame'}, dimensions={1} | all-to-all | bytes 3538944 | tf_op jit(solution)/shard_map/all_to_all | solution.py:262
  1287.7 83.3 %reduce-scatter.35.cloned.1.call-done = f32[1,4,64,1152]{3,2,1,0:T(8,128)} async-done(((f32[1,4,256,1152]{3,2,1,0:T(8,128)}), f32[1,4,64,1152]{3,2,1,0:T(8,128)}) %reduce-scatter.35.cloned.1.call-update) | async-done | bytes 1179664 | tf_op jit(solution)/shard_map/reduce_scatter | solution.py:150
  1376.9 51.1 %all-gather.45.cloned.1.call-done = bf16[1,4,256,1152]{3,2,1,0:T(8,128)(2,1)} async-done(((bf16[1,4,64,1152]{3,2,1,0:T(8,128)(2,1)}), bf16[1,4,256,1152]{3,2,1,0:T(8,128)(2,1)}) %all-gather.45.cloned.1.call-update) | async-done | bytes 2359312 | tf_op jit(solution)/shard_map/all_gather | solution.py:146
  1442.3 84.2 %reduce-scatter.37.cloned.1.call-done = f32[1,4,64,1152]{3,2,1,0:T(8,128)} async-done(((f32[1,4,256,1152]{3,2,1,0:T(8,128)}), f32[1,4,64,1152]{3,2,1,0:T(8,128)}) %reduce-scatter.37.cloned.1.call-update) | async-done | bytes 1179664 | tf_op jit(solution)/shard_map/reduce_scatter | solution.py:150
  1532.8 50.7 %all-gather.47.cloned.1.call-done = bf16[1,4,256,1152]{3,2,1,0:T(8,128)(2,1)} async-done(((bf16[1,4,64,1152]{3,2,1,0:T(8,128)(2,1)}), bf16[1,4,256,1152]{3,2,1,0:T(8,128)(2,1)}) %all-gather.47.cloned.1.call-update) | async-done | bytes 2359312 | tf_op jit(solution)/shard_map/all_gather | solution.py:146
  1600.2 82.2 %reduce-scatter.39.cloned.1.call-done = f32[1,4,64,1152]{3,2,1,0:T(8,128)} async-done(((f32[1,4,256,1152]{3,2,1,0:T(8,128)}), f32[1,4,64,1152]{3,2,1,0:T(8,128)}) %reduce-scatter.39.cloned.1.call-update) | async-done | bytes 1179664 | tf_op jit(solution)/shard_map/reduce_scatter | solution.py:150
  1778.3 45.6 %reduce-scatter.59.cloned.1.call-done = bf16[1152,144]{0,1:T(8,128)(2,1)} async-done(((bf16[1152,1152]{0,1:T(8,128)(2,1)}), bf16[1152,144]{0,1:T(8,128)(2,1)}) %reduce-scatter.59.cloned.1.call-update) | async-done | bytes 331792 | tf_op jit(solution)/shard_map/reduce_scatter | solution.py:301
  1825.8 37.0 %reduce-scatter.55.cloned.1.call-done = bf16[288,144]{0,1:T(8,128)(2,1)} async-done(((bf16[288,1152]{0,1:T(8,128)(2,1)}), bf16[288,144]{0,1:T(8,128)(2,1)}) %reduce-scatter.55.cloned.1.call-update) | async-done | bytes 82960 | tf_op jit(solution)/shard_map/reduce_scatter | solution.py:295
  1864.4 46.1 %reduce-scatter.53.cloned.1.call-done = bf16[144,3,288]{2,0,1:T(8,128)(2,1)} async-done(((bf16[1152,3,288]{2,0,1:T(8,128)(2,1)}), bf16[144,3,288]{2,0,1:T(8,128)(2,1)}) %reduce-scatter.53.cloned.1.call-update) | async-done | bytes 248848 | tf_op jit(solution)/shard_map/reduce_scatter | solution.py:292
  1912.3 42.0 %all-gather.51.cloned.1.call-done = bf16[1152,6,288]{2,0,1:T(8,128)(2,1)} async-done(((bf16[144,6,288]{2,0,1:T(8,128)(2,1)}), bf16[1152,6,288]{2,0,1:T(8,128)(2,1)}) %all-gather.51.cloned.1.call-update) | async-done | bytes 3981328 | tf_op jit(solution)/shard_map/all_gather | solution.py:137
  1961.1 40.3 %reduce-scatter.49.cloned.1.call-done = bf16[1152,144]{0,1:T(8,128)(2,1)} async-done(((bf16[1152,1152]{0,1:T(8,128)(2,1)}), bf16[1152,144]{0,1:T(8,128)(2,1)}) %reduce-scatter.49.cloned.1.call-update) | async-done | bytes 331792 | tf_op jit(solution)/shard_map/reduce_scatter | solution.py:301
  2003.3 45.8 %reduce-scatter.47.cloned.1.call-done = bf16[144,1152]{1,0:T(8,128)(2,1)} async-done(((bf16[1152,1152]{1,0:T(8,128)(2,1)}), bf16[144,1152]{1,0:T(8,128)(2,1)}) %reduce-scatter.47.cloned.1.call-update) | async-done | bytes 331792 | tf_op jit(solution)/shard_map/reduce_scatter | solution.py:298
  2051.0 37.1 %reduce-scatter.45.cloned.1.call-done = bf16[288,144]{0,1:T(8,128)(2,1)} async-done(((bf16[288,1152]{0,1:T(8,128)(2,1)}), bf16[288,144]{0,1:T(8,128)(2,1)}) %reduce-scatter.45.cloned.1.call-update) | async-done | bytes 82960 | tf_op jit(solution)/shard_map/reduce_scatter | solution.py:295
  2089.7 45.9 %reduce-scatter.43.cloned.1.call-done = bf16[144,3,288]{2,0,1:T(8,128)(2,1)} async-done(((bf16[1152,3,288]{2,0,1:T(8,128)(2,1)}), bf16[144,3,288]{2,0,1:T(8,128)(2,1)}) %reduce-scatter.43.cloned.1.call-update) | async-done | bytes 248848 | tf_op jit(solution)/shard_map/reduce_scatter | solution.py:292
  2139.0 40.6 %all-gather.49.cloned.1.call-done = bf16[1152,6,288]{2,0,1:T(8,128)(2,1)} async-done(((bf16[144,6,288]{2,0,1:T(8,128)(2,1)}), bf16[1152,6,288]{2,0,1:T(8,128)(2,1)}) %all-gather.49.cloned.1.call-update) | async-done | bytes 3981328 | tf_op jit(solution)/shard_map/all_gather | solution.py:137
  2186.3 34.9 %psum.7 = f32[1,1152]{1,0:T(1,128)S(1)} all-reduce(f32[1,1152]{1,0:T(1,128)S(1)} %add.301), channel_id=1, replica_groups=mesh['clip'=2,'frame'=4,'tensor'=4] {'frame','tensor'}, use_global_device_ids=true, to_apply=%region_44.45 | all-reduce | flops 1152 | bytes 9216 | tf_op jit(solution)/shard_map/psum | solution.py:341
  2242.6 58.4 %reduce-scatter.51.cloned.1.call-done = bf16[144,6,288]{2,0,1:T(8,128)(2,1)} async-done(((bf16[1152,6,288]{2,0,1:T(8,128)(2,1)}), bf16[144,6,288]{2,0,1:T(8,128)(2,1)}) %reduce-scatter.51.cloned.1.call-update) | async-done | bytes 497680 | tf_op jit(solution)/shard_map/reduce_scatter | solution.py:289
  (478 shorter events, 598.2 us)
Async XLA Ops:
  7.2 174.9 %all-gather.23.cloned.1.call-start = ((), (), s32[]{:S(2)}) async-start(), calls=%async_computation.25 | async-start | bytes 2985984 | tf_op jit(solution)/shard_map/all_gather | solution.py:127
  83.9 138.8 %all-gather.21.cloned.1.call-start = ((), (), s32[]{:S(2)}) async-start(), calls=%async_computation.24 | async-start | bytes 2949120 | tf_op jit(solution)/shard_map/all_gather | solution.py:146
  171.1 148.5 %reduce-scatter.25.cloned.1.call-start = ((), (), s32[]{:S(2)}) async-start(), calls=%async_computation.26 | async-start | bytes 5898240 | tf_op jit(solution)/shard_map/reduce_scatter | solution.py:150
  235.3 117.4 %all-gather.27.cloned.1.call-start = ((), (), s32[]{:S(2)}) async-start(), calls=%async_computation.28 | async-start | bytes 2985984 | tf_op jit(solution)/shard_map/all_gather | solution.py:129
  237.2 168.0 %all-gather.25.cloned.1.call-start = ((), (), s32[]{:S(2)}) async-start(), calls=%async_computation.27 | async-start | bytes 2949120 | tf_op jit(solution)/shard_map/all_gather | solution.py:146
  323.5 208.9 %reduce-scatter.27.cloned.1.call-start = ((), (), s32[]{:S(2)}) async-start(), calls=%async_computation.30 | async-start | bytes 5898240 | tf_op jit(solution)/shard_map/reduce_scatter | solution.py:150
  446.2 119.4 %all-gather.33.cloned.1.call-start = ((), (), s32[]{:S(2)}) async-start(), calls=%async_computation.32 | async-start | bytes 2985984 | tf_op jit(solution)/shard_map/all_gather | solution.py:127
  452.2 166.0 %all-gather.31.cloned.1.call-start = ((), (), s32[]{:S(2)}) async-start(), calls=%async_computation.31 | async-start | bytes 2949120 | tf_op jit(solution)/shard_map/all_gather | solution.py:146
  704.4 116.8 %all-gather.37.cloned.1.call-start = ((), (), s32[]{:S(2)}) async-start(), calls=%async_computation.35 | async-start | bytes 2985984 | tf_op jit(solution)/shard_map/all_gather | solution.py:129
  706.4 167.3 %all-gather.35.cloned.1.call-start = ((), (), s32[]{:S(2)}) async-start(), calls=%async_computation.34 | async-start | bytes 2949120 | tf_op jit(solution)/shard_map/all_gather | solution.py:146
  793.5 164.2 %all-gather.41.cloned.1.call-start = ((), (), s32[]{:S(2)}) async-start(), calls=%async_computation.38 | async-start | bytes 2949120 | tf_op jit(solution)/shard_map/all_gather | solution.py:146
  795.6 260.7 %reduce-scatter.33.cloned.1.call-start = ((), (), s32[]{:S(2)}) async-start(), calls=%async_computation.39 | async-start | bytes 5898240 | tf_op jit(solution)/shard_map/reduce_scatter | solution.py:150
  972.0 172.2 %reduce-scatter.31.cloned.1.call-start = ((), (), s32[]{:S(2)}) async-start(), calls=%async_computation.37 | async-start | bytes 5898240 | tf_op jit(solution)/shard_map/reduce_scatter | solution.py:150
  981.7 220.3 %all-gather.43.cloned.1.call-start = ((), (), s32[]{:S(2)}) async-start(), calls=%async_computation.40 | async-start | bytes 2949120 | tf_op jit(solution)/shard_map/all_gather | solution.py:146
  1212.0 159.0 %reduce-scatter.35.cloned.1.call-start = ((), (), s32[]{:S(2)}) async-start(), calls=%async_computation.41 | async-start | bytes 5898240 | tf_op jit(solution)/shard_map/reduce_scatter | solution.py:150
  1287.6 140.3 %all-gather.45.cloned.1.call-start = ((), (), s32[]{:S(2)}) async-start(), calls=%async_computation.42 | async-start | bytes 2949120 | tf_op jit(solution)/shard_map/all_gather | solution.py:146
  1376.8 149.7 %reduce-scatter.37.cloned.1.call-start = ((), (), s32[]{:S(2)}) async-start(), calls=%async_computation.43 | async-start | bytes 5898240 | tf_op jit(solution)/shard_map/reduce_scatter | solution.py:150
  1442.2 141.2 %all-gather.47.cloned.1.call-start = ((), (), s32[]{:S(2)}) async-start(), calls=%async_computation.44 | async-start | bytes 2949120 | tf_op jit(solution)/shard_map/all_gather | solution.py:146
  1532.3 150.1 %reduce-scatter.39.cloned.1.call-start = ((), (), s32[]{:S(2)}) async-start(), calls=%async_computation.45 | async-start | bytes 5898240 | tf_op jit(solution)/shard_map/reduce_scatter | solution.py:150
  1598.1 148.1 %reduce-scatter.63.cloned.1.call-start = ((), (), s32[]{:S(2)}) async-start(), calls=%async_computation.59 | async-start | bytes 737280
  1600.1 147.1 %reduce-scatter.61.cloned.1.call-start = ((), (), s32[]{:S(2)}) async-start(), calls=%async_computation.58 | async-start | bytes 737280
  1693.4 130.6 %reduce-scatter.59.cloned.1.call-start = ((), (), s32[]{:S(2)}) async-start(), calls=%async_computation.57 | async-start | bytes 2985984 | tf_op jit(solution)/shard_map/reduce_scatter | solution.py:301
  1701.6 161.1 %reduce-scatter.55.cloned.1.call-start = ((), (), s32[]{:S(2)}) async-start(), calls=%async_computation.55 | async-start | bytes 995328 | tf_op jit(solution)/shard_map/reduce_scatter | solution.py:295
  1706.8 203.7 %reduce-scatter.53.cloned.1.call-start = ((), (), s32[]{:S(2)}) async-start(), calls=%async_computation.54 | async-start | bytes 2985984 | tf_op jit(solution)/shard_map/reduce_scatter | solution.py:292
  1714.0 240.3 %all-gather.51.cloned.1.call-start = ((), (), s32[]{:S(2)}) async-start(), calls=%async_computation.47 | async-start | bytes 5971968 | tf_op jit(solution)/shard_map/all_gather | solution.py:137
  1716.3 285.1 %reduce-scatter.49.cloned.1.call-start = ((), (), s32[]{:S(2)}) async-start(), calls=%async_computation.52 | async-start | bytes 2985984 | tf_op jit(solution)/shard_map/reduce_scatter | solution.py:301
  1724.4 324.7 %reduce-scatter.47.cloned.1.call-start = ((), (), s32[]{:S(2)}) async-start(), calls=%async_computation.51 | async-start | bytes 2985984 | tf_op jit(solution)/shard_map/reduce_scatter | solution.py:298
  1731.8 356.3 %reduce-scatter.45.cloned.1.call-start = ((), (), s32[]{:S(2)}) async-start(), calls=%async_computation.50 | async-start | bytes 995328 | tf_op jit(solution)/shard_map/reduce_scatter | solution.py:295
  1736.9 398.7 %reduce-scatter.43.cloned.1.call-start = ((), (), s32[]{:S(2)}) async-start(), calls=%async_computation.49 | async-start | bytes 2985984 | tf_op jit(solution)/shard_map/reduce_scatter | solution.py:292
  1743.8 435.7 %all-gather.49.cloned.1.call-start = ((), (), s32[]{:S(2)}) async-start(), calls=%async_computation.46 | async-start | bytes 5971968 | tf_op jit(solution)/shard_map/all_gather | solution.py:137
  1746.1 494.3 %reduce-scatter.41.cloned.1.call-start = ((), (), s32[]{:S(2)}) async-start(), calls=%async_computation.48 | async-start | bytes 5971968 | tf_op jit(solution)/shard_map/reduce_scatter | solution.py:289
  1755.1 545.9 %reduce-scatter.51.cloned.1.call-start = ((), (), s32[]{:S(2)}) async-start(), calls=%async_computation.53 | async-start | bytes 5971968 | tf_op jit(solution)/shard_map/reduce_scatter | solution.py:289
  (113 other events, 4460.6 us)
Sparse Core Ops, SparseCore 0:
  84.0 41.4 all-gather.22
  171.2 51.4 all-gather.20
  235.4 84.0 reduce-scatter.24
  321.9 30.7 all-gather.26
  354.7 50.4 all-gather.24
  446.3 85.9 reduce-scatter.26
  534.8 30.7 all-gather.32
  567.7 50.4 all-gather.30
  704.6 83.3 reduce-scatter.28
  790.4 30.7 all-gather.36
  823.2 50.4 all-gather.34
  907.3 50.4 all-gather.40
  972.2 84.0 reduce-scatter.32
  1058.4 85.7 reduce-scatter.30
  1151.0 50.9 all-gather.42
  1287.8 83.1 reduce-scatter.34
  1376.9 50.9 all-gather.44
  1442.4 84.0 reduce-scatter.36
  1532.4 50.9 all-gather.46
  1598.3 84.0 reduce-scatter.38
  1734.3 42.1 reduce-scatter.56
  1780.2 43.7 reduce-scatter.58
  1827.6 35.1 reduce-scatter.54
  1866.7 43.7 reduce-scatter.52
  1912.9 41.3 all-gather.50
  1957.7 43.7 reduce-scatter.48
  2005.4 43.7 reduce-scatter.46
  2052.9 35.1 reduce-scatter.44
  2091.8 43.7 reduce-scatter.42
  2138.1 41.3 all-gather.48
  2183.0 57.3 reduce-scatter.40
  2243.8 57.2 reduce-scatter.50
  (4 shorter events, 100.7 us)
